TPU v7x, 128 devices: a whole 4x4x4 slice. The times are simulated.
128 devices in a mesh: member: 8 (over y, core), dp: 16 (over z, x).
Axes of the slice: x: 4, y: 4, z: 4, core: 2. Of those that a mesh axis runs over, the one named last changes fastest.
Arguments:
- observations: bfloat16 [4096, 1152], P(('member', 'dp')), may hold values from -6 to 6
- rollout: bfloat16 [4096, 384], P(('member', 'dp')), as said below
- done_flags: int32 [4096, 24], P(('member', 'dp')), may hold values 0 or 1
- member_ids: int32 [4096, 1], P(('member', 'dp')), may hold values from 0 to 15; in each aligned block of 32 rows (0 to 31, 32 to 63, ...) at most 6 rows name the same one
- embed_weight: float32 [16, 48, 256], P('member'), may hold values from -0.875 to 0.875
- conv_weight: float32 [16, 3, 2, 256, 256], P('member'), may hold values from -0.25 to 0.25
- trunk_in: float32 [16, 256, 512], P('member'), may hold values from -0.375 to 0.375
- trunk_mid: float32 [16, 512, 512], P('member'), may hold values from -0.25 to 0.25
- head_weight: float32 [16, 512, 13], P('member'), may hold values from -0.15625 to 0.15625
- log_std: float32 [16, 12], P('member'), may hold values from -0.1 to 0.1
Outputs:
- embed_dir: float32 [16, 48, 256], P('member', 'dp')
- conv_dir: float32 [16, 3, 2, 256, 256], P('member', None, None, 'dp')
- in_dir: float32 [16, 256, 512], P('member', 'dp')
- mid_dir: float32 [16, 512, 512], P('member', 'dp')
- head_dir: float32 [16, 512, 13], P('member', 'dp')
- std_dir: float32 [16, 12], P('member')
Inputs may be any that keep to these rules, and one draw needn't show every extreme that they name: `member_ids`: in each shard's 32 rows no member is named more than 6 times, a bound that some block reaches. `rollout`: per step: 12 action values, reward, old value, next value, old log-probability.
All inputs are finite; a program needn't handle non-finite values. No bound on the sum of `done_flags` on one device may be relied on, other than what follows from the above.
Results may differ from a plain program's by a relative error of at most 0.023.
Values may be sent and summed in bfloat16 or wider, within the bound.
No kernel may reach another device: no remote copies, remote signals or barrier semaphores. Data moves between devices by JAX's collectives and lax.ppermute only.
A program may use at most 128 MiB of HBM per device.

v0:
```python
import jax
import jax.numpy as jnp
from jax import lax
from jax.experimental import pallas as pl
from jax.experimental.pallas import tpu as pltpu
from jax.sharding import Mesh, PartitionSpec as P


gamma_rate = 0.99
trace_rate = 0.95
half_log_tau = 0.9189385332046727

OBS = 48
STEPS = 24
ACT = 12
CH = 256
UNITS = 512
MEMBERS = 16
CAP = 6
SLOT = 8
REC = 64
WIDTH = STEPS * REC
ENTRIES = 805388
SOURCES = 16
SPANS = SOURCES * CAP
CHUNK_STEPS = 8
CHUNKS = STEPS // CHUNK_STEPS
ROWS = CHUNK_STEPS * SPANS
ALL_ROWS = STEPS * SPANS
PAD = 4 * SPANS
SHARDS = 16
HALF = 104
W_MID, W_IN, W_EMBED, W_HEAD, W_ROWS = 1536, 2560, 3072, 3328, 3360
f32 = jnp.float32
bf16 = jnp.bfloat16


def iota(shape, dim):
    return lax.broadcasted_iota(jnp.int32, shape, dim)


def dot(a, b):
    return jnp.dot(a, b, preferred_element_type=f32)


def dot_tn(a, b):
    return lax.dot_general(a, b, (((0,), (0,)), ((), ())), preferred_element_type=f32)


def dot_nt(a, b):
    return lax.dot_general(a, b, (((1,), (1,)), ((), ())), preferred_element_type=f32)


def onehot(cond):
    return jnp.where(cond, 1.0, 0.0).astype(bf16)


def pack_kernel(
    which_ref, obs_hbm, roll_hbm, done_hbm, ids_hbm, embed_hbm, conv_hbm, in_hbm, mid_hbm, head_hbm,
    out_hbm, w_hbm,
    out_ref, w_ref, obs_ref, roll_ref, done_ref, ids_ref, embed_ref, conv_ref, in_ref, mid_ref, head_ref,
    pick_ref, obs_at, act_at, scal_at, sems,
):
    which = which_ref[0]
    sources = [roll_hbm, done_hbm, obs_hbm, ids_hbm, head_hbm]
    sources += [conv_hbm.at[which], mid_hbm.at[which], in_hbm.at[which], embed_hbm.at[which]]
    targets = [roll_ref, done_ref, obs_ref, ids_ref, head_ref, conv_ref, mid_ref, in_ref, embed_ref]
    copies = [
        pltpu.make_async_copy(source, target, sems.at[k]) for k, (source, target) in enumerate(zip(sources, targets))
    ]
    moves, head_move, (conv_move, mid_move, in_move, embed_move) = copies[:4], copies[4], copies[5:]
    for move in copies:
        move.start()

    def store(k, start, stop):
        return pltpu.make_async_copy(w_ref.at[start:stop], w_hbm.at[start:stop], sems.at[k])

    stores = [pltpu.make_async_copy(out_ref, out_hbm, sems.at[9])]
    stores += [store(10, 0, W_MID), store(11, W_MID, W_IN), store(12, W_IN, W_ROWS)]
    spans = obs_ref.shape[0]
    col = iota((1, 512), 1)
    spot, within, step = col & 63, col >> 6, col & 127
    row = iota((384, 512), 0)
    obs_at[...] = onehot(row == jnp.where(spot < 48, 48 * within + spot, -1))
    act_at[...] = onehot(row[0:128] == jnp.where((spot >= 48) & (spot < 60), 16 * within + spot - 48, -1))
    scal_at[...] = onehot(row == jnp.where((spot >= 60) & (spot < 63), (spot - 60) * 128 + within, -1))
    pick_ref[...] = onehot(row == jnp.where(step < STEPS, 16 * step + 12 + (col >> 7), -1))
    for move in moves:
        move.wait()
    parts = dot(roll_ref[...], pick_ref[...])
    reward, old_value = parts[:, 0:128], parts[:, 128:256]
    next_value, old_logp = parts[:, 256:384], parts[:, 384:512]
    widen = onehot(iota((STEPS, 128), 0) == iota((STEPS, 128), 1))
    done = dot_tn(done_ref[...].astype(f32).astype(bf16), widen)
    lane = iota((spans, 128), 1)
    alive = jnp.where(lane < STEPS, 1.0 - done, 0.0)
    advantage = reward + gamma_rate * alive * next_value - old_value
    carry = gamma_rate * trace_rate * alive
    for shift in (1, 2, 4, 8, 16):
        advantage = advantage + carry * pltpu.roll(advantage, 128 - shift, 1)
        carry = carry * pltpu.roll(carry, 128 - shift, 1)
    target = jnp.where(lane < STEPS, advantage + old_value, 0.0)
    advantage = jnp.where(lane < STEPS, advantage, 0.0)
    scalars = [target, advantage, old_logp]

    live = jnp.where((iota((spans, 512), 1) & 63) == 63, 1.0, 0.0)
    groups = []
    for g in range(3):
        placed = dot(obs_ref[:, 384 * g : 384 * g + 384], obs_at[...])
        placed = placed + dot(roll_ref[:, 128 * g : 128 * g + 128], act_at[...])
        turned = [pltpu.roll(x, (128 - 8 * g) % 128, 1) if g else x for x in scalars]
        turned = jnp.concatenate([x.astype(bf16) for x in turned], axis=1)
        placed = placed + dot(turned, scal_at[...]) + live
        groups.append(placed.astype(bf16))

    slots = MEMBERS * SLOT
    ids = ids_ref[...]
    slot, span = iota((slots, spans), 0), iota((slots, spans), 1)
    named = onehot(iota((MEMBERS, spans), 0) == ids)
    earlier = onehot(iota((spans, spans), 0) < iota((spans, spans), 1))
    rank = jnp.sum(dot(named, earlier) * named.astype(f32), axis=0, keepdims=True)
    dispatch = onehot(slot == ids * SLOT + rank.astype(jnp.int32))
    for g in range(3):
        out_ref[:, 512 * g : 512 * g + 512] = dot(dispatch, groups[g]).astype(bf16)
    stores[0].start()

    halves = (slice(0, 256), slice(256, 512))
    head_move.wait()
    head = jnp.where(which == 0, head_ref[:, 0, :], head_ref[:, 1, :]).astype(bf16)
    head = dot(onehot(iota((16, ACT + 1), 0) == iota((16, ACT + 1), 1)), head).astype(bf16)
    for n in range(2):
        w_ref[W_HEAD + 16 * n : W_HEAD + 16 * n + 16, :] = head[:, halves[n]]
    conv_move.wait()
    for layer in range(3):
        for tap in range(2):
            at = CH * (2 * layer + tap)
            w_ref[at : at + CH, :] = conv_ref[layer, tap].astype(bf16)
    stores[1].start()
    mid_move.wait()
    for n in range(2):
        w_ref[W_MID + UNITS * n : W_MID + UNITS * n + UNITS, :] = mid_ref[:, halves[n]].astype(bf16)
    stores[2].start()
    in_move.wait()
    for n in range(2):
        w_ref[W_IN + CH * n : W_IN + CH * n + CH, :] = in_ref[:, halves[n]].astype(bf16)
    embed_move.wait()
    embed = embed_ref[...].astype(bf16)
    r, k = iota((128, OBS), 0), iota((128, OBS), 1)
    for n in range(2):
        w_ref[W_EMBED + 128 * n : W_EMBED + 128 * n + 128, :] = dot(onehot(r == k + REC * n), embed).astype(bf16)
    stores[3].start()
    for move in stores:
        move.wait()


def pack(which, observations, rollout, done_flags, member_ids, embed, conv, trunk_in, trunk_mid, head):
    v = pltpu.VMEM
    spans = (observations, rollout, done_flags.T, member_ids.T)
    weights = (embed, conv, trunk_in, trunk_mid)
    head = head.transpose(2, 0, 1)
    return pl.pallas_call(
        pack_kernel,
        out_shape=(jax.ShapeDtypeStruct((MEMBERS * SLOT, WIDTH), bf16), jax.ShapeDtypeStruct((W_ROWS, CH), bf16)),
        in_specs=[pl.BlockSpec(memory_space=pltpu.SMEM)] + [pl.BlockSpec(memory_space=pltpu.HBM)] * 9,
        out_specs=(pl.BlockSpec(memory_space=pltpu.HBM), pl.BlockSpec(memory_space=pltpu.HBM)),
        scratch_shapes=[v((MEMBERS * SLOT, WIDTH), bf16), v((W_ROWS, CH), bf16)]
        + [v(x.shape, x.dtype) for x in spans]
        + [v(x.shape[1:], f32) for x in weights]
        + [v(head.shape, f32)]
        + [v((384, 512), bf16), v((384, 512), bf16), v((128, 512), bf16), v((384, 512), bf16)]
        + [pltpu.SemaphoreType.DMA((13,))],
        compiler_params=pltpu.CompilerParams(vmem_limit_bytes=60 * 1024 * 1024),
        name="pack",
    )(which, *spans, *weights, head)


def grad_kernel(
    which_ref, own_ref, core_ref, recv_ref, w_ref, scale_ref, other_ref,
    keep_ref, give_ref, stat_ref,
    xc, xt, hid, c0, c1, c2, c3, g0, g1, g2, first, second, dout, dp2, dp1, dhid, dm0, dm1, dm2, dpair,
    acc_conv, acc_in, acc_mid, acc_head, acc_stat,
):
    own = own_ref[0] == 1
    cs, gs, dms = (c0, c1, c2), (g0, g1, g2), (dm0, dm1, dm2)
    for ref in cs:
        ref[0:PAD, :] = jnp.zeros((PAD, CH), bf16)
    for ref in dms:
        ref[ALL_ROWS : ALL_ROWS + PAD, :] = jnp.zeros((PAD, CH), bf16)

    r, k = iota((SPANS, SOURCES * SLOT), 0), iota((SPANS, SOURCES * SLOT), 1)
    compact = onehot(((k & 7) < CAP) & (r == (k >> 3) * CAP + (k & 7)))
    r, k = iota((64, 128), 0), iota((64, 128), 1)
    entry = r & 31
    select = onehot((entry < 16) & (k == entry + OBS + (r >> 5) * REC))
    sub = iota((16, 1), 0)
    is_act = sub < ACT
    scale = jnp.where(own, scale_ref[...], other_ref[...])
    scale = jnp.where(which_ref[0] == 0, scale[0:1, :], scale[1:2, :])
    log_scale = jnp.sum(jnp.where(iota((16, ACT), 0) == iota((16, ACT), 1), scale, 0.0), axis=1, keepdims=True)
    conv = [w_ref.at[2 * CH * layer : 2 * CH * layer + 2 * CH] for layer in range(3)]
    in_half = [w_ref.at[W_IN + CH * n : W_IN + CH * n + CH] for n in range(2)]
    mid_half = [w_ref.at[W_MID + UNITS * n : W_MID + UNITS * n + UNITS] for n in range(2)]
    embed_half = [w_ref.at[W_EMBED + 128 * n : W_EMBED + 128 * n + 128] for n in range(2)]
    head_half = [w_ref.at[W_HEAD + 16 * n : W_HEAD + 16 * n + 16] for n in range(2)]

    def across(halves, rows):
        return jnp.concatenate([half[rows, :] for half in halves], axis=1)

    inverse = jnp.where(is_act, jnp.exp(-log_scale), 0.0)
    offset = jnp.sum(jnp.where(is_act, log_scale, 0.0), axis=0, keepdims=True) + ACT * half_log_tau
    lane = iota((1, ROWS), 1)
    odd = lane < 0
    for s in range(1, CHUNK_STEPS, 2):
        odd = odd | ((lane >= s * SPANS) & (lane < (s + 1) * SPANS))

    pairs = CHUNK_STEPS // 2
    blocks = (0, 256)

    def rows(i, shift=0):
        return slice(i * ROWS + shift, (i + 1) * ROWS + shift)

    def add(ref, at, value, start):
        if start:
            ref[at] = value
        else:
            ref[at] += value

    def elu(x):
        below = jnp.minimum((jnp.exp(x) - 1.0).astype(bf16), jnp.zeros((), bf16))
        return jnp.maximum(x.astype(bf16), below)

    def slope(y):
        return jnp.minimum(y, jnp.zeros((), bf16)) + jnp.ones((), bf16)

    def forward(i):
        def enter():
            x = dot(compact, recv_ref[:, i * pairs * 128 : (i + 1) * pairs * 128]).astype(bf16)
            for p in range(pairs):
                part = x[:, 128 * p : 128 * p + 128]
                at = i * (ROWS // 2) + p * SPANS
                xc[at : at + SPANS, :] = part
                for half in range(2):
                    at = i * ROWS + (2 * p + half) * SPANS
                    xt[at : at + SPANS, :] = part
            y = [dot(xc[i * (ROWS // 2) : (i + 1) * (ROWS // 2), :], half[...]) for half in embed_half]
            for p in range(pairs):
                for half in range(2):
                    at = i * ROWS + (2 * p + half) * SPANS
                    h = y[half][p * SPANS : (p + 1) * SPANS, :]
                    hid[at - i * ROWS : at - i * ROWS + SPANS, :] = h
                    c0[PAD + at : PAD + at + SPANS, :] = h.astype(bf16)

        def encode(layer):
            c, lag = cs[layer], SPANS * 2**layer
            both = jnp.concatenate([c[rows(i, PAD), :], c[rows(i, PAD - lag), :]], axis=1)
            mix = dot(both, conv[layer][...])
            grown = jnp.exp(mix)
            h = hid[...] + jnp.maximum(mix, jnp.minimum(grown - 1.0, 0.0))
            gs[layer][rows(i), :] = grown.astype(bf16)
            if layer < 2:
                hid[...] = h
                cs[layer + 1][rows(i, PAD), :] = h.astype(bf16)
            else:
                c3[rows(i), :] = h.astype(bf16)

        def widen(n):
            first[rows(i), n : n + 256] = elu(dot(c3[rows(i), :], in_half[n // 256][...]))

        def deepen(n):
            second[rows(i), n : n + 256] = elu(dot(first[rows(i), :], mid_half[n // 256][...]))

        yield enter
        for layer in range(3):
            yield lambda layer=layer: encode(layer)
        for n in blocks:
            yield lambda n=n: widen(n)
        for n in blocks:
            yield lambda n=n: deepen(n)

    def backward(i):
        def loss():
            out = dot_nt(across(head_half, slice(0, 16)), second[rows(i), :])
            record = dot_nt(select, xt[rows(i), :])
            record = jnp.where(odd, record[32:64], record[0:32])
            diff = record[0:16] - out
            scaled = diff * inverse
            square = scaled * scaled
            advantage, old_logp, live = record[13:14], record[14:15], record[15:16]
            log_ratio = -0.5 * jnp.sum(square, axis=0, keepdims=True) - offset - old_logp
            ratio = jnp.exp(log_ratio)
            dlog = live * (0.5 * (ratio - 1.0) - ratio * advantage)
            dvalue = -0.5 * live * diff
            d = jnp.where(sub == ACT, dvalue, dlog * scaled * inverse)
            dout[...] = d.astype(bf16)
            total = jnp.sum(dlog * (square - 1.0), axis=1, keepdims=True)
            add(acc_stat, Ellipsis, jnp.broadcast_to(total, acc_stat.shape), i == 0)

        def down(n):
            ds = dot_tn(dout[...], head_half[n // 256][...])
            dp2[:, n : n + 256] = ds.astype(bf16) * slope(second[rows(i), n : n + 256])

        def head():
            add(acc_head, Ellipsis, dot(dout[...], second[rows(i), :]), i == 0)

        def middle(n):
            df = dot_nt(dp2[...], across(mid_half, slice(n, n + 256)))
            dp1[:, n : n + 256] = df.astype(bf16) * slope(first[rows(i), n : n + 256])

        def top():
            dhid[rows(i), :] = dot_nt(dp1[...], across(in_half, slice(0, CH)))

        def grad_mid():
            add(acc_mid, Ellipsis, dot_tn(first[rows(i), :], dp2[...]), i == 0)

        def grad_in():
            add(acc_in, Ellipsis, dot_tn(c3[rows(i), :], dp1[...]), i == 0)

        yield loss
        for n in blocks:
            yield lambda n=n: down(n)
        yield head
        for n in blocks:
            yield lambda n=n: middle(n)
        yield top
        yield grad_mid
        yield grad_in

    def decode(i):
        start = i == CHUNKS - 1
        for layer in (2, 1, 0):
            c, dm, lag = cs[layer], dms[layer], SPANS * 2**layer
            dh = dhid[rows(i), :]
            dm[rows(i), :] = dh.astype(bf16) * jnp.minimum(gs[layer][rows(i), :], jnp.ones((), bf16))
            dc = dot_nt(dm[rows(i), :], conv[layer][0:256, :])
            dc = dc + dot_nt(dm[rows(i, lag), :], conv[layer][256:512, :])
            dh = dh + dc
            if layer > 0:
                dhid[rows(i), :] = dh
            else:
                for s in range(CHUNK_STEPS):
                    at = i * (ROWS // 2) + (s // 2) * SPANS
                    part = dh[s * SPANS : s * SPANS + SPANS].astype(bf16)
                    dpair[at : at + SPANS, 256 * (s % 2) : 256 * (s % 2) + 256] = part
            both = jnp.concatenate([c[rows(i, PAD), :], c[rows(i, PAD - lag), :]], axis=1)
            add(acc_conv, layer, dot_tn(both, dm[rows(i), :]), start)

    def weave(left, right):
        left, right = list(left), list(right)
        order = [((k + 0.5) / len(left), 0, f) for k, f in enumerate(left)]
        order += [((k + 0.5) / len(right), 1, f) for k, f in enumerate(right)]
        for _, _, run in sorted(order, key=lambda item: item[:2]):
            run()

    weave(forward(0), [])
    for i in range(1, CHUNKS):
        weave(forward(i), backward(i - 1))
    weave(backward(CHUNKS - 1), [])
    for i in range(CHUNKS - 1, -1, -1):
        decode(i)

    dembed = dot_tn(xc[...], dpair[...])
    dembed = (dembed[0:OBS, 0:256] + dembed[REC : REC + OBS, 256:512]).astype(bf16)
    r, k = iota((SHARDS * 8, OBS), 0), iota((SHARDS * 8, OBS), 1)
    spread = onehot(((r & 7) < 3) & (k == (r >> 3) * 3 + (r & 7)))
    extra = dot(spread, dembed).astype(bf16)
    dhead = acc_head[...].astype(bf16)

    def write(encoder_ref, trunk_ref):
        for s in range(SHARDS):
            for q in range(6):
                encoder_ref[s, 16 * q : 16 * q + 16, :] = acc_conv[q // 2, 256 * (q % 2) + 16 * s : 256 * (q % 2) + 16 * s + 16, :].astype(bf16)
            encoder_ref[s, 96:104, :] = extra[8 * s : 8 * s + 8, :]
            for n in range(2):
                cols = slice(256 * n, 256 * n + 256)
                trunk_ref[s, 16 * n : 16 * n + 16, :] = acc_in[16 * s : 16 * s + 16, cols].astype(bf16)
                trunk_ref[s, 32 + 32 * n : 64 + 32 * n, :] = acc_mid[32 * s : 32 * s + 32, cols].astype(bf16)
            trunk_ref[s, 96:104, :] = jnp.zeros((8, 256), bf16)
            for n in range(2):
                trunk_ref[s, 96:104, 32 * n : 32 * n + 32] = dhead[8 * n : 8 * n + 8, 32 * s : 32 * s + 32]

    @pl.when(core_ref[0] == 0)
    def _():
        write(keep_ref, give_ref)

    @pl.when(core_ref[0] == 1)
    def _():
        write(give_ref, keep_ref)

    at = (iota((16, 128), 0) == iota((16, 128), 1)) & is_act
    line = jnp.sum(jnp.where(at, acc_stat[...], 0.0), axis=0, keepdims=True)
    stat_ref[...] = jnp.broadcast_to(line, (8, 128))


def member_grad(which, own, core, recv, weights, scale, other):
    v = pltpu.VMEM
    half = ALL_ROWS // 2
    return pl.pallas_call(
        grad_kernel,
        out_shape=(
            jax.ShapeDtypeStruct((SHARDS, HALF, 256), bf16),
            jax.ShapeDtypeStruct((SHARDS, HALF, 256), bf16),
            jax.ShapeDtypeStruct((8, 128), f32),
        ),
        in_specs=[pl.BlockSpec(memory_space=pltpu.SMEM)] * 3 + [pl.BlockSpec(memory_space=v)] * 4,
        scratch_shapes=[
            v((half, 128), bf16), v((ALL_ROWS, 128), bf16), v((ROWS, CH), f32),
            v((PAD + ALL_ROWS, CH), bf16), v((PAD + ALL_ROWS, CH), bf16), v((PAD + ALL_ROWS, CH), bf16),
            v((ALL_ROWS, CH), bf16),
            v((ALL_ROWS, CH), bf16), v((ALL_ROWS, CH), bf16), v((ALL_ROWS, CH), bf16),
            v((ALL_ROWS, UNITS), bf16), v((ALL_ROWS, UNITS), bf16), v((16, ROWS), bf16),
            v((ROWS, UNITS), bf16), v((ROWS, UNITS), bf16),
            v((ALL_ROWS, CH), f32),
            v((ALL_ROWS + PAD, CH), bf16), v((ALL_ROWS + PAD, CH), bf16), v((ALL_ROWS + PAD, CH), bf16),
            v((half, 512), bf16),
            v((3, 2 * CH, CH), f32), v((CH, UNITS), f32), v((UNITS, UNITS), f32), v((16, UNITS), f32), v((16, 128), f32),
        ],
        cost_estimate=pl.CostEstimate(flops=11_200_000_000, bytes_accessed=4_000_000, transcendentals=4_000_000),
        compiler_params=pltpu.CompilerParams(vmem_limit_bytes=42 * 1024 * 1024),
        name="grad",
    )(which, own, core, recv, weights, scale, other)


def reduce_kernel(core_ref, recv_ref, stat_ref, mine_ref, theirs_ref, cast_ref):
    lane1 = iota((1, 128), 1)
    line = pltpu.roll(stat_ref[0:1, :], 32, 1)
    for whose, out_ref in ((core_ref[0], mine_ref), (1 - core_ref[0], theirs_ref)):
        for j in range(2):
            kind = 2 * whose + j
            total = recv_ref[kind].astype(f32)
            for z in range(1, 4):
                total = total + recv_ref[4 * z + kind].astype(f32)
            out_ref[j] = total
            line = line + jnp.where(lane1 == kind, jnp.sum(total * total), 0.0)
    for s in range(2 * SHARDS):
        cast_ref[8 * s : 8 * s + 8, :] = jnp.broadcast_to(line, (8, 128))


def reduce_parts(core, recv, stat):
    part = jax.ShapeDtypeStruct((2, HALF, 256), f32)
    return pl.pallas_call(
        reduce_kernel,
        out_shape=(part, part, jax.ShapeDtypeStruct((2 * SHARDS * 8, 128), f32)),
        in_specs=[pl.BlockSpec(memory_space=pltpu.SMEM)] + [pl.BlockSpec(memory_space=pltpu.VMEM)] * 2,
        compiler_params=pltpu.CompilerParams(vmem_limit_bytes=16 * 1024 * 1024),
        name="reduce",
    )(core, recv, stat)


def finish_kernel(core_ref, mine_ref, theirs_ref, lines_ref, embed_ref, conv_ref, in_ref, mid_ref, head_ref, std_ref):
    core = core_ref[0]
    lane1 = iota((1, 128), 1)
    total = jnp.sum(lines_ref[...], axis=0, keepdims=True) * 0.125
    scales = []
    for j in range(2):
        kind = 2 * core + j
        std = jnp.zeros((1, 128), f32)
        for z in range(8):
            at = pl.ds(pl.multiple_of(8 * (4 * z + kind), 8), 8)
            std = std + lines_ref[at, :][0:1]
        std = jnp.where((lane1 >= 32) & (lane1 < 32 + ACT), std, 0.0)
        square = jnp.sum(std * std + jnp.where(lane1 == kind, total, 0.0), axis=1, keepdims=True)
        scale = 1.0 / jnp.sqrt(square / ENTRIES + 1e-06)
        std_ref[j : j + 1, :] = (std * scale)[:, 32 : 32 + ACT]
        scales.append(scale)

    def write(encoder_ref, trunk_ref):
        for j, scale in enumerate(scales):
            for q in range(6):
                conv_ref[j, q // 2, q % 2] = encoder_ref[j, 16 * q : 16 * q + 16, :] * scale
            embed_ref[:, j, :] = encoder_ref[j, 96:99, :] * scale
            for n in range(2):
                cols = slice(256 * n, 256 * n + 256)
                in_ref[j, :, cols] = trunk_ref[j, 16 * n : 16 * n + 16, :] * scale
                mid_ref[j, :, cols] = trunk_ref[j, 32 + 32 * n : 64 + 32 * n, :] * scale
            head_ref[0:8, j, :] = trunk_ref[j, 96:104, 0:32] * scale
            head_ref[8:13, j, :] = trunk_ref[j, 96:101, 32:64] * scale

    @pl.when(core == 0)
    def _():
        write(mine_ref, theirs_ref)

    @pl.when(core == 1)
    def _():
        write(theirs_ref, mine_ref)


def finish(core, mine, theirs, lines):
    shapes = ((3, 2, 256), (2, 3, 2, 16, 256), (2, 16, 512), (2, 32, 512), (13, 2, 32), (2, 12))
    embed, conv, first, second, head, std = pl.pallas_call(
        finish_kernel,
        out_shape=tuple(jax.ShapeDtypeStruct(s, f32) for s in shapes),
        in_specs=[pl.BlockSpec(memory_space=pltpu.SMEM)] + [pl.BlockSpec(memory_space=pltpu.VMEM)] * 3,
        compiler_params=pltpu.CompilerParams(vmem_limit_bytes=16 * 1024 * 1024),
        name="finish",
    )(core, mine, theirs, lines)
    return embed.transpose(1, 0, 2), conv, first, second, head.transpose(1, 2, 0), std


def swap(value):
    return lax.ppermute(value, "core", [(0, 1), (1, 0)])


def local(observations, rollout, done_flags, member_ids, embed_weight, conv_weight, trunk_in, trunk_mid, head_weight, log_std):
    x, core = lax.axis_index("x"), lax.axis_index("core")
    which, own = (x % 2).reshape(1), (core == x // 2).astype(jnp.int32).reshape(1)
    core = core.reshape(1)
    packed, weights = pack(
        which, observations, rollout, done_flags, member_ids, embed_weight, conv_weight, trunk_in, trunk_mid, head_weight
    )
    far = swap(weights)
    recv = lax.all_to_all(packed, ("y", "x"), split_axis=0, concat_axis=0, tiled=True)
    other = swap(log_std)
    weights = jnp.where(own[0] == 1, weights, far)
    keep, give, stat = member_grad(which, own, core, recv, weights, log_std, other)
    both = (keep.astype(f32) + swap(give).astype(f32)).astype(bf16)
    parts = lax.all_to_all(both, ("z", "x"), split_axis=0, concat_axis=0, tiled=True)
    mine, theirs, cast = reduce_parts(core, parts, stat)
    lines = lax.all_to_all(cast, ("core", "z", "x"), split_axis=0, concat_axis=0, tiled=True)
    theirs = swap(theirs)
    return finish(core, mine, theirs, lines)


def solution(mesh):
    fine = Mesh(mesh.devices.reshape(4, 2, 4, 4), ("y", "core", "z", "x"))
    member, dp = ("y", "core"), ("z", "x")
    every = member + dp
    return jax.shard_map(
        local,
        mesh=fine,
        in_specs=(P(every), P(every), P(every), P(every)) + (P(member),) * 6,
        out_specs=(
            P(member, dp),
            P(member, None, None, dp),
            P(member, dp),
            P(member, dp),
            P(member, dp),
            P(member),
        ),
        check_vma=False,
    )
```

profile of v0, /device:TPU:0, one launch (start us, length us, event | category | flops | bytes accessed | tf_op | source)
XLA Modules:
  0.0 74.5 jit_solution(16344488397101872562)
XLA Ops:
  0.6 0.0 copy-start
  0.7 3.8 %pack.1 = (bf16[128,1536]{1,0:T(8,128)(2,1)}, bf16[3360,256]{1,0:T(8,128)(2,1)}) custom-call(s32[1]{0:T(128)} %bitcast.1.which_ref, bf16[32,1152]{1,0:T(8,128)(2,1)} %obs_hbm.1, bf16[32,384]{1,0:T(8,128)(2,1)} %roll_hbm.1, s32[24,32]{1,0:T(8,128)} %bitcast.17, s32[1,32]{1,0:T(1,128)} %bitcast.18, f32[2,48,256]{2,1,0:T(8,128)} %embed_hbm.1, ...), custom_call_target="tpu_custom_call" | custom-call | tf_op jit(solution)/shard_map/pack/pallas_call | solution.py:161
  4.4 0.1 collective-permute-start
  4.5 7.2 %all-to-all-start = ((bf16[16,8,1536]{2,1,0:T(8,128)(2,1)}), bf16[16,8,1536]{2,1,0:T(8,128)(2,1)S(1)}, u32[]{:S(2)}, u32[]{:S(2)}) async-start(bf16[16,8,1536]{2,1,0:T(8,128)(2,1)} %bitcast.15), calls=%async_computation | async-start | bytes 786432 | tf_op jit(solution)/shard_map/all_to_all | solution.py:511
  11.7 0.0 copy-done
  11.7 0.3 collective-permute-start.1
  12.0 0.0 collective-permute-done
  12.0 1.6 %broadcast_select_fusion.w_ref = bf16[3360,256]{1,0:T(8,128)(2,1)S(1)} fusion(bf16[3360,256]{1,0:T(8,128)(2,1)} %get-tuple-element.21, bf16[3360,256]{1,0:T(8,128)(2,1)} %collective-permute-done, pred[]{:T(512)S(6)} %eq.9), kind=kLoop, calls=%fused_computation | loop fusion | flops 860160 | bytes 5160961 | tf_op jit(solution)/shard_map/jit(_where)/select_n | solution.py:513
  13.6 0.0 collective-permute-done.1.other_ref
  13.6 8.8 %all-to-all-done = bf16[16,8,1536]{2,1,0:T(8,128)(2,1)S(1)} async-done(((bf16[16,8,1536]{2,1,0:T(8,128)(2,1)}), bf16[16,8,1536]{2,1,0:T(8,128)(2,1)S(1)}, u32[]{:S(2)}, u32[]{:S(2)}) %all-to-all-start) | async-done | bytes 393248 | tf_op jit(solution)/shard_map/all_to_all | solution.py:511
  22.4 16.1 %grad.1 = (bf16[16,104,256]{2,1,0:T(8,128)(2,1)S(1)}, bf16[16,104,256]{2,1,0:T(8,128)(2,1)S(1)}, f32[8,128]{1,0:T(8,128)S(1)}) custom-call(s32[1]{0:T(128)} %bitcast.1.which_ref, s32[1]{0:T(128)} %bitcast.2.own_ref, s32[1]{0:T(128)} %bitcast.core_ref, bf16[128,1536]{1,0:T(8,128)(2,1)S(1)} %bitcast.13, bf16[3360,256]{1,0:T(8,128)(2,1)S(1)} %broadcast_select_fusion.w_ref, ...), custom_call_target="tpu_custom_call" | custom-call | flops 11200000000 | bytes 4000000 | tf_op jit(solution)/shard_map/grad/pallas_call | solution.py:397
  38.5 0.1 collective-permute-start.2
  38.6 2.4 %collective-permute-done.2 = bf16[16,104,256]{2,1,0:T(8,128)(2,1)S(1)} collective-permute-done((bf16[16,104,256]{2,1,0:T(8,128)(2,1)S(1)}, bf16[16,104,256]{2,1,0:T(8,128)(2,1)S(1)}, u32[]{:S(2)}, u32[]{:S(2)}) %collective-permute-start.2) | collective-permute-done | bytes 852000 | tf_op jit(solution)/shard_map/ppermute | solution.py:500
  41.0 0.3 add_convert_fusion
  41.2 20.9 %all_to_all.27.recv_ref = bf16[16,104,256]{2,1,0:T(8,128)(2,1)S(1)} all-to-all(bf16[16,104,256]{2,1,0:T(8,128)(2,1)S(1)} %add_convert_fusion), channel_id=1, replica_groups=mesh['y'=4,'core'=2,'z'=4,'x'=4] {'z','x'}, dimensions={0} | all-to-all | bytes 1703936 | tf_op jit(solution)/shard_map/all_to_all | solution.py:516
  62.1 0.3 reduce.1
  62.4 0.1 collective-permute-start.3
  62.5 11.0 %all_to_all.28 = f32[32,8,128]{2,1,0:T(8,128)S(1)} all-to-all(f32[32,8,128]{2,1,0:T(8,128)S(1)} %bitcast.14), channel_id=1, replica_groups=mesh['y'=4,'core'=2,'z'=4,'x'=4] {'core','z','x'}, dimensions={0} | all-to-all | bytes 262144 | tf_op jit(solution)/shard_map/all_to_all | solution.py:518
  73.5 0.0 collective-permute-done.3.theirs_ref
  73.5 1.0 %finish.1 = (f32[3,2,256]{2,1,0:T(2,128)}, f32[2,3,2,16,256]{4,3,2,1,0:T(8,128)}, f32[2,16,512]{2,1,0:T(8,128)}, f32[2,32,512]{2,1,0:T(8,128)}, f32[13,2,32]{2,1,0:T(2,128)}, /*index=5*/f32[2,12]{1,0:T(2,128)}) custom-call(s32[1]{0:T(128)} %bitcast.core_ref, f32[2,104,256]{2,1,0:T(8,128)S(1)} %get-tuple-element.25.mine_ref, ...), custom_call_target="tpu_custom_call" | custom-call | tf_op jit(solution)/shard_map/finish/pallas_call | solution.py:489
Async XLA Ops:
  0.6 11.0 %copy-start = (f32[2,12]{1,0:T(2,128)S(1)}, f32[2,12]{1,0:T(2,128)}, u32[]{:S(2)}) copy-start(f32[2,12]{1,0:T(2,128)} %scale_ref.1) | copy-start | bytes 292
  4.4 7.6 %collective-permute-start = (bf16[3360,256]{1,0:T(8,128)(2,1)}, bf16[3360,256]{1,0:T(8,128)(2,1)}, u32[]{:S(2)}, u32[]{:S(2)}) collective-permute-start(bf16[3360,256]{1,0:T(8,128)(2,1)} %get-tuple-element.21), channel_id=1, source_target_pairs={{0,16},{16,0},{1,17},{17,1},{2,18},{18,2},{3,19},{19,3},{4,20},{20... | collective-permute-start | bytes 5160968 | tf_op jit(solution)/shard_map/ppermute | solution.py:500
  4.5 17.9 %all-to-all-start = ((bf16[16,8,1536]{2,1,0:T(8,128)(2,1)}), bf16[16,8,1536]{2,1,0:T(8,128)(2,1)S(1)}, u32[]{:S(2)}, u32[]{:S(2)}) async-start(bf16[16,8,1536]{2,1,0:T(8,128)(2,1)} %bitcast.15), calls=%async_computation | async-start | bytes 786432 | tf_op jit(solution)/shard_map/all_to_all | solution.py:511
  11.7 1.9 %collective-permute-start.1 = (f32[2,12]{1,0:T(2,128)S(1)}, f32[2,12]{1,0:T(2,128)S(1)}, u32[]{:S(2)}, u32[]{:S(2)}) collective-permute-start(f32[2,12]{1,0:T(2,128)S(1)} %copy-done), channel_id=1, source_target_pairs={{0,16},{16,0},{1,17},{17,1},{2,18},{18,2},{3,19},{19,3},{4,20},{20... | collective-permute-start | bytes 296 | tf_op jit(solution)/shard_map/ppermute | solution.py:500
  38.5 2.5 %collective-permute-start.2 = (bf16[16,104,256]{2,1,0:T(8,128)(2,1)S(1)}, bf16[16,104,256]{2,1,0:T(8,128)(2,1)S(1)}, u32[]{:S(2)}, u32[]{:S(2)}) collective-permute-start(bf16[16,104,256]{2,1,0:T(8,128)(2,1)S(1)} %get-tuple-element.23), channel_id=1, source_target_pairs={{0,16},{16,0},{1,17},{17,1},{2,18},{18,2},{3,19},{19,3},{4,20},{20... | collective-permute-start | bytes 2555912 | tf_op jit(solution)/shard_map/ppermute | solution.py:500
  62.4 11.1 %collective-permute-start.3 = (f32[2,104,256]{2,1,0:T(8,128)S(1)}, f32[2,104,256]{2,1,0:T(8,128)S(1)}, u32[]{:S(2)}, u32[]{:S(2)}) collective-permute-start(f32[2,104,256]{2,1,0:T(8,128)S(1)} %get-tuple-element.26), channel_id=1, source_target_pairs={{0,16},{16,0},{1,17},{17,1},{2,18},{18,2},{3,19},{19,3},{4,20},{20... | collective-permute-start | bytes 638984 | tf_op jit(solution)/shard_map/ppermute | solution.py:500
where the time goes:
time: 75.7 us; the launch traced here: 74.5 us
  blocking collectives  31.9 us (42%)
  Pallas kernels  21.1 us (28%)
  waiting for transfers between devices  11.2 us (15%)
  starting transfers between devices  7.71 us (10%)
  other arithmetic  1.91 us (3%)
    all_to_all x1, blocking collectives, local(): lax.all_to_all(both, ('z', 'x'), split_axis=0, concat_axis=0, tiled=True)  20.9 us
    pallas_call x1, Pallas kernels, member_grad(): pl.pallas_call(grad_kernel, out_shape=(jax.ShapeDtypeStruct((SHARDS, HALF...  16.1 us
    all_to_all x1, blocking collectives, local(): lax.all_to_all(cast, ('core', 'z', 'x'), split_axis=0, concat_axis=0, til...  11 us
    all_to_all x1, waiting for transfers between devices, local(): lax.all_to_all(packed, ('y', 'x'), split_axis=0, concat_axis=0, tiled=True)  8.78 us
    all_to_all x1, starting transfers between devices, local(): lax.all_to_all(packed, ('y', 'x'), split_axis=0, concat_axis=0, tiled=True)  7.17 us
    pallas_call x1, Pallas kernels, pack(): pl.pallas_call(pack_kernel, out_shape=(jax.ShapeDtypeStruct((MEMBERS * SL...  3.76 us
    ppermute x4, waiting for transfers between devices, swap(): return lax.ppermute(value, 'core', [(0, 1), (1, 0)])  2.37 us
    select_n x1, other arithmetic, local(): weights = jnp.where(own[0] == 1, weights, far)  1.64 us
  transfers between devices with their start and end apart: 5, of which 2 were waited for; matrix products, arithmetic and copies ran while one was open for 2% of the time, Pallas kernels for 0%

commit v1 on v0

--- a/solution.py
+++ b/solution.py
@@ -432,14 +432,14 @@
             out_ref[j] = total
             line = line + jnp.where(lane1 == kind, jnp.sum(total * total), 0.0)
     for s in range(2 * SHARDS):
-        cast_ref[8 * s : 8 * s + 8, :] = jnp.broadcast_to(line, (8, 128))
+        cast_ref[s] = line
 
 
 def reduce_parts(core, recv, stat):
     part = jax.ShapeDtypeStruct((2, HALF, 256), f32)
     return pl.pallas_call(
         reduce_kernel,
-        out_shape=(part, part, jax.ShapeDtypeStruct((2 * SHARDS * 8, 128), f32)),
+        out_shape=(part, part, jax.ShapeDtypeStruct((2 * SHARDS, 1, 128), f32)),
         in_specs=[pl.BlockSpec(memory_space=pltpu.SMEM)] + [pl.BlockSpec(memory_space=pltpu.VMEM)] * 2,
         compiler_params=pltpu.CompilerParams(vmem_limit_bytes=16 * 1024 * 1024),
         name="reduce",
@@ -449,14 +449,13 @@
 def finish_kernel(core_ref, mine_ref, theirs_ref, lines_ref, embed_ref, conv_ref, in_ref, mid_ref, head_ref, std_ref):
     core = core_ref[0]
     lane1 = iota((1, 128), 1)
-    total = jnp.sum(lines_ref[...], axis=0, keepdims=True) * 0.125
+    total = jnp.sum(lines_ref[...], axis=0)
     scales = []
     for j in range(2):
         kind = 2 * core + j
         std = jnp.zeros((1, 128), f32)
         for z in range(8):
-            at = pl.ds(pl.multiple_of(8 * (4 * z + kind), 8), 8)
-            std = std + lines_ref[at, :][0:1]
+            std = std + lines_ref[4 * z + kind]
         std = jnp.where((lane1 >= 32) & (lane1 < 32 + ACT), std, 0.0)
         square = jnp.sum(std * std + jnp.where(lane1 == kind, total, 0.0), axis=1, keepdims=True)
         scale = 1.0 / jnp.sqrt(square / ENTRIES + 1e-06)
@@ -516,8 +515,7 @@
     parts = lax.all_to_all(both, ("z", "x"), split_axis=0, concat_axis=0, tiled=True)
     mine, theirs, cast = reduce_parts(core, parts, stat)
     lines = lax.all_to_all(cast, ("core", "z", "x"), split_axis=0, concat_axis=0, tiled=True)
-    theirs = swap(theirs)
-    return finish(core, mine, theirs, lines)
+    return finish(core, mine, swap(theirs), lines)
 
 
 def solution(mesh):

time: 75.7 us -> 75.1 us (level)
  no operation moved by 1% of the time
where the time goes in v1:
time: 75.1 us; the launch traced here: 74.1 us
  blocking collectives  31.4 us (42%)
  Pallas kernels  21.1 us (28%)
  waiting for transfers between devices  11.2 us (15%)
  starting transfers between devices  7.71 us (10%)
  other arithmetic  1.91 us (3%)
    all_to_all x1, blocking collectives, local(): lax.all_to_all(both, ('z', 'x'), split_axis=0, concat_axis=0, tiled=True)  20.9 us
    pallas_call x1, Pallas kernels, member_grad(): pl.pallas_call(grad_kernel, out_shape=(jax.ShapeDtypeStruct((SHARDS, HALF...  16.1 us
    all_to_all x1, blocking collectives, local(): lax.all_to_all(cast, ('core', 'z', 'x'), split_axis=0, concat_axis=0, til...  10.6 us
    all_to_all x1, waiting for transfers between devices, local(): lax.all_to_all(packed, ('y', 'x'), split_axis=0, concat_axis=0, tiled=True)  8.78 us
    all_to_all x1, starting transfers between devices, local(): lax.all_to_all(packed, ('y', 'x'), split_axis=0, concat_axis=0, tiled=True)  7.17 us
    pallas_call x1, Pallas kernels, pack(): pl.pallas_call(pack_kernel, out_shape=(jax.ShapeDtypeStruct((MEMBERS * SL...  3.76 us
    ppermute x4, waiting for transfers between devices, swap(): return lax.ppermute(value, 'core', [(0, 1), (1, 0)])  2.37 us
    select_n x1, other arithmetic, local(): weights = jnp.where(own[0] == 1, weights, far)  1.64 us
  transfers between devices with their start and end apart: 5, of which 2 were waited for; matrix products, arithmetic and copies ran while one was open for 2% of the time, Pallas kernels for 0%

profile of v1, /device:TPU:0, one launch (start us, length us, event | category | flops | bytes accessed | tf_op | source)
XLA Modules:
  0.0 74.1 jit_solution(10438226373648493705)
XLA Ops:
  0.6 0.0 copy-start
  0.7 3.8 %pack.1 = (bf16[128,1536]{1,0:T(8,128)(2,1)}, bf16[3360,256]{1,0:T(8,128)(2,1)}) custom-call(s32[1]{0:T(128)} %bitcast.1.which_ref, bf16[32,1152]{1,0:T(8,128)(2,1)} %obs_hbm.1, bf16[32,384]{1,0:T(8,128)(2,1)} %roll_hbm.1, s32[24,32]{1,0:T(8,128)} %bitcast.13, s32[1,32]{1,0:T(1,128)} %bitcast.14, f32[2,48,256]{2,1,0:T(8,128)} %embed_hbm.1, ...), custom_call_target="tpu_custom_call" | custom-call | tf_op jit(solution)/shard_map/pack/pallas_call | solution.py:161
  4.4 0.1 collective-permute-start
  4.5 7.2 %all-to-all-start = ((bf16[16,8,1536]{2,1,0:T(8,128)(2,1)}), bf16[16,8,1536]{2,1,0:T(8,128)(2,1)S(1)}, u32[]{:S(2)}, u32[]{:S(2)}) async-start(bf16[16,8,1536]{2,1,0:T(8,128)(2,1)} %bitcast.11), calls=%async_computation | async-start | bytes 786432 | tf_op jit(solution)/shard_map/all_to_all | solution.py:510
  11.7 0.0 copy-done
  11.7 0.3 collective-permute-start.1
  12.0 0.0 collective-permute-done
  12.0 1.6 %broadcast_select_fusion.w_ref = bf16[3360,256]{1,0:T(8,128)(2,1)S(1)} fusion(bf16[3360,256]{1,0:T(8,128)(2,1)} %get-tuple-element.21, bf16[3360,256]{1,0:T(8,128)(2,1)} %collective-permute-done, pred[]{:T(512)S(6)} %eq.9), kind=kLoop, calls=%fused_computation | loop fusion | flops 860160 | bytes 5160961 | tf_op jit(solution)/shard_map/jit(_where)/select_n | solution.py:512
  13.6 0.0 collective-permute-done.1.other_ref
  13.6 8.8 %all-to-all-done = bf16[16,8,1536]{2,1,0:T(8,128)(2,1)S(1)} async-done(((bf16[16,8,1536]{2,1,0:T(8,128)(2,1)}), bf16[16,8,1536]{2,1,0:T(8,128)(2,1)S(1)}, u32[]{:S(2)}, u32[]{:S(2)}) %all-to-all-start) | async-done | bytes 393248 | tf_op jit(solution)/shard_map/all_to_all | solution.py:510
  22.4 16.1 %grad.1 = (bf16[16,104,256]{2,1,0:T(8,128)(2,1)S(1)}, bf16[16,104,256]{2,1,0:T(8,128)(2,1)S(1)}, f32[8,128]{1,0:T(8,128)S(1)}) custom-call(s32[1]{0:T(128)} %bitcast.1.which_ref, s32[1]{0:T(128)} %bitcast.2.own_ref, s32[1]{0:T(128)} %bitcast.core_ref, bf16[128,1536]{1,0:T(8,128)(2,1)S(1)} %bitcast.10, bf16[3360,256]{1,0:T(8,128)(2,1)S(1)} %broadcast_select_fusion.w_ref, ...), custom_call_target="tpu_custom_call" | custom-call | flops 11200000000 | bytes 4000000 | tf_op jit(solution)/shard_map/grad/pallas_call | solution.py:397
  38.5 0.1 collective-permute-start.2
  38.6 2.4 %collective-permute-done.2 = bf16[16,104,256]{2,1,0:T(8,128)(2,1)S(1)} collective-permute-done((bf16[16,104,256]{2,1,0:T(8,128)(2,1)S(1)}, bf16[16,104,256]{2,1,0:T(8,128)(2,1)S(1)}, u32[]{:S(2)}, u32[]{:S(2)}) %collective-permute-start.2) | collective-permute-done | bytes 852000 | tf_op jit(solution)/shard_map/ppermute | solution.py:499
  41.0 0.3 add_convert_fusion
  41.2 20.9 %all_to_all.21.recv_ref = bf16[16,104,256]{2,1,0:T(8,128)(2,1)S(1)} all-to-all(bf16[16,104,256]{2,1,0:T(8,128)(2,1)S(1)} %add_convert_fusion), channel_id=1, replica_groups=mesh['y'=4,'core'=2,'z'=4,'x'=4] {'z','x'}, dimensions={0} | all-to-all | bytes 1703936 | tf_op jit(solution)/shard_map/all_to_all | solution.py:515
  62.1 0.3 reduce.1
  62.4 0.1 collective-permute-start.3
  62.5 10.6 %all_to_all.22.lines_ref = f32[32,1,128]{2,1,0:T(1,128)S(1)} all-to-all(f32[32,1,128]{2,1,0:T(1,128)S(1)} %get-tuple-element.27), channel_id=1, replica_groups=mesh['y'=4,'core'=2,'z'=4,'x'=4] {'core','z','x'}, dimensions={0} | all-to-all | bytes 32768 | tf_op jit(solution)/shard_map/all_to_all | solution.py:517
  73.0 0.0 collective-permute-done.3.theirs_ref
  73.0 1.0 %finish.1 = (f32[3,2,256]{2,1,0:T(2,128)}, f32[2,3,2,16,256]{4,3,2,1,0:T(8,128)}, f32[2,16,512]{2,1,0:T(8,128)}, f32[2,32,512]{2,1,0:T(8,128)}, f32[13,2,32]{2,1,0:T(2,128)}, /*index=5*/f32[2,12]{1,0:T(2,128)}) custom-call(s32[1]{0:T(128)} %bitcast.core_ref, f32[2,104,256]{2,1,0:T(8,128)S(1)} %get-tuple-element.25.mine_ref, ...), custom_call_target="tpu_custom_call" | custom-call | tf_op jit(solution)/shard_map/finish/pallas_call | solution.py:488
Async XLA Ops:
  0.6 11.0 %copy-start = (f32[2,12]{1,0:T(2,128)S(1)}, f32[2,12]{1,0:T(2,128)}, u32[]{:S(2)}) copy-start(f32[2,12]{1,0:T(2,128)} %scale_ref.1) | copy-start | bytes 292
  4.4 7.6 %collective-permute-start = (bf16[3360,256]{1,0:T(8,128)(2,1)}, bf16[3360,256]{1,0:T(8,128)(2,1)}, u32[]{:S(2)}, u32[]{:S(2)}) collective-permute-start(bf16[3360,256]{1,0:T(8,128)(2,1)} %get-tuple-element.21), channel_id=1, source_target_pairs={{0,16},{16,0},{1,17},{17,1},{2,18},{18,2},{3,19},{19,3},{4,20},{20... | collective-permute-start | bytes 5160968 | tf_op jit(solution)/shard_map/ppermute | solution.py:499
  4.5 17.9 %all-to-all-start = ((bf16[16,8,1536]{2,1,0:T(8,128)(2,1)}), bf16[16,8,1536]{2,1,0:T(8,128)(2,1)S(1)}, u32[]{:S(2)}, u32[]{:S(2)}) async-start(bf16[16,8,1536]{2,1,0:T(8,128)(2,1)} %bitcast.11), calls=%async_computation | async-start | bytes 786432 | tf_op jit(solution)/shard_map/all_to_all | solution.py:510
  11.7 1.9 %collective-permute-start.1 = (f32[2,12]{1,0:T(2,128)S(1)}, f32[2,12]{1,0:T(2,128)S(1)}, u32[]{:S(2)}, u32[]{:S(2)}) collective-permute-start(f32[2,12]{1,0:T(2,128)S(1)} %copy-done), channel_id=1, source_target_pairs={{0,16},{16,0},{1,17},{17,1},{2,18},{18,2},{3,19},{19,3},{4,20},{20... | collective-permute-start | bytes 296 | tf_op jit(solution)/shard_map/ppermute | solution.py:499
  38.5 2.5 %collective-permute-start.2 = (bf16[16,104,256]{2,1,0:T(8,128)(2,1)S(1)}, bf16[16,104,256]{2,1,0:T(8,128)(2,1)S(1)}, u32[]{:S(2)}, u32[]{:S(2)}) collective-permute-start(bf16[16,104,256]{2,1,0:T(8,128)(2,1)S(1)} %get-tuple-element.23), channel_id=1, source_target_pairs={{0,16},{16,0},{1,17},{17,1},{2,18},{18,2},{3,19},{19,3},{4,20},{20... | collective-permute-start | bytes 2555912 | tf_op jit(solution)/shard_map/ppermute | solution.py:499
  62.4 10.7 %collective-permute-start.3 = (f32[2,104,256]{2,1,0:T(8,128)S(1)}, f32[2,104,256]{2,1,0:T(8,128)S(1)}, u32[]{:S(2)}, u32[]{:S(2)}) collective-permute-start(f32[2,104,256]{2,1,0:T(8,128)S(1)} %get-tuple-element.26), channel_id=1, source_target_pairs={{0,16},{16,0},{1,17},{17,1},{2,18},{18,2},{3,19},{19,3},{4,20},{20... | collective-permute-start | bytes 638984 | tf_op jit(solution)/shard_map/ppermute | solution.py:499
